TPU v7x, 256 devices: a whole 4x4x8 slice. The times are simulated.
256 devices in a mesh: rows: 128 (over x, z, y), cols: 2 (over core).
Axes of the slice: x: 4, y: 4, z: 8, core: 2. Of those that a mesh axis runs over, the one named last changes fastest.
Arguments:
- embeddings: bfloat16 [262144, 384], P('rows')
- test_matrix: bfloat16 [262144, 64], P('rows'), may hold values from -6 to 6
- pair_list: int32 [1024, 2], P(('rows', 'cols')), may hold values from -1 to 255, as said below
Outputs:
- orthonormal_basis: float32 [262144, 64], P(('rows', 'cols'))
- upper_factor: float32 [64, 64], replicated
Inputs may be any that keep to these rules, and one draw needn't show every extreme that they name: `pair_list`: device (r, c) holds 4 entries. Its live entries come first: pairs (i, j) with r * 2 <= i < (r + 1) * 2 and i <= j < min((r + 3) * 2, 256); each pair appears at most once over all devices; its other entries are -1 in both places. The device with c = 0 holds at least one live pair, the two devices of one r hold at most 4 together, and device (0, 0) holds exactly 4.
All inputs are finite; a program needn't handle non-finite values.
Results may differ from a plain program's by a relative error of at most 0.0053.
Values may be sent and summed in bfloat16 or wider, within the bound.
No kernel may reach another device: no remote copies, remote signals or barrier semaphores. Data moves between devices by JAX's collectives and lax.ppermute only.
A program may use at most 64 MiB of HBM per device.

v0:
```python
import jax
import jax.numpy as jnp
from jax import lax
from jax.sharding import PartitionSpec as P

BLK = 1024
SHARPNESS = 6.0
EPSILON = 1e-06


def shifted(value, axis, steps):
    count = lax.axis_size(axis)
    initial, last = (max(0, -steps), min(count, count - steps))
    return lax.ppermute(value, axis, [(source, source + steps) for source in range(initial, last)])


def unit_rows(embeddings):
    widened = embeddings.astype(jnp.float32)
    inverse = lax.rsqrt(jnp.sum(widened * widened, axis=1, keepdims=True) + EPSILON)
    return (widened * inverse).astype(jnp.bfloat16)


def affinity(left_rows, right_rows):
    scores = lax.dot_general(
        left_rows, right_rows, (((1,), (1,)), ((), ())), preferred_element_type=jnp.float32
    )
    return jnp.exp(SHARPNESS * (scores - 1.0)).astype(jnp.bfloat16)


def mirror_product(affinity_tile, vectors):
    return lax.dot_general(
        affinity_tile, vectors, (((0,), (0,)), ((), ())), preferred_element_type=jnp.float32
    )


def block_at(stacked, index):
    return lax.dynamic_index_in_dim(stacked, index, 0, keepdims=False)


def add_block(stacked, index, term):
    return lax.dynamic_update_index_in_dim(stacked, block_at(stacked, index) + term, index, 0)


def count_live(pair_rows):
    return jnp.sum((pair_rows[:, 0] >= 0).astype(jnp.int32))


def orthonormal(sketch_rows, rows_total):
    gram_matrix = lax.dot_general(
        sketch_rows,
        sketch_rows,
        (((0,), (0,)), ((), ())),
        precision=lax.Precision.HIGHEST,
        preferred_element_type=jnp.float32,
    )
    gram_matrix = lax.psum(gram_matrix, ("rows", "cols")) / rows_total
    lower_factor = jnp.linalg.cholesky(gram_matrix)
    solved = lax.linalg.triangular_solve(
        lower_factor, sketch_rows, left_side=False, lower=True, transpose_a=True
    )
    return (solved, lower_factor.T)


def affinity_pass(window_units, own_vectors, my_pairs, base_block):
    blocks_dev = own_vectors.shape[0]
    ahead_vectors = [shifted(own_vectors, "rows", -offset) for offset in (1, 2)]
    window_vectors = jnp.concatenate([own_vectors] + ahead_vectors, axis=0)
    initial = jnp.zeros(window_vectors.shape, jnp.float32)

    def pair_step(slot_index, accumulated):
        entry = my_pairs[slot_index]
        first_block = entry[0] - base_block
        second_block = entry[1] - base_block
        affinity_tile = affinity(
            block_at(window_units, first_block), block_at(window_units, second_block)
        )
        forward = jnp.dot(
            affinity_tile,
            block_at(window_vectors, second_block),
            preferred_element_type=jnp.float32,
        )
        accumulated = add_block(accumulated, first_block, forward)
        mirrored = first_block != second_block

        def add_mirror(current):
            return add_block(
                current,
                second_block,
                mirror_product(affinity_tile, block_at(window_vectors, first_block)),
            )

        return lax.cond(mirrored, add_mirror, lambda unchanged: unchanged, accumulated)

    accumulated = lax.fori_loop(0, count_live(my_pairs), pair_step, initial)
    own_blocks = accumulated[:blocks_dev]
    for offset in (1, 2):
        own_blocks = own_blocks + shifted(
            accumulated[offset * blocks_dev : (offset + 1) * blocks_dev], "rows", offset
        )
    flattened = own_blocks.reshape(-1, own_blocks.shape[2])
    return lax.psum_scatter(flattened, "cols", scatter_dimension=0, tiled=True)


def local(embeddings, test_matrix, pair_list):
    rows_dev = embeddings.shape[0]
    blocks_dev = rows_dev // BLK
    columns = test_matrix.shape[1]
    base_block = lax.axis_index("rows") * blocks_dev
    rows_total = rows_dev * lax.axis_size("rows")
    normed = unit_rows(embeddings).reshape(blocks_dev, BLK, embeddings.shape[1])
    ahead_units = [shifted(normed, "rows", -offset) for offset in (1, 2)]
    window_units = jnp.concatenate([normed] + ahead_units, axis=0)
    sketch_rows = affinity_pass(
        window_units, test_matrix.reshape(blocks_dev, BLK, columns), pair_list, base_block
    )
    panel_rows, _ = orthonormal(sketch_rows, rows_total)
    panel_whole = lax.all_gather(panel_rows.astype(jnp.bfloat16), "cols", axis=0, tiled=True)
    image_rows = affinity_pass(
        window_units, panel_whole.reshape(blocks_dev, BLK, columns), pair_list, base_block
    )
    return orthonormal(image_rows, rows_total)


def solution(mesh):
    in_specs = (P("rows", None), P("rows", None), P(("rows", "cols"), None))
    out_specs = (P(("rows", "cols"), None), P())
    return jax.shard_map(local, mesh=mesh, in_specs=in_specs, out_specs=out_specs, check_vma=False)
```

profile of v0, /device:TPU:1, one launch (start us, length us, event | category | flops | bytes accessed | tf_op | source)
XLA Modules:
  0.0 547.8 jit_solution(13680197383918252103)
XLA Ops:
  7.2 1.9 fusion.32
  9.5 1.3 collective-permute-start
  15.7 85.9 %collective-permute-done.2 = bf16[2,1024,64]{2,1,0:T(8,128)(2,1)S(1)} collective-permute-done((bf16[2,1024,64]{2,1,0:T(8,128)(2,1)S(1)}, bf16[2,1024,64]{2,1,0:T(8,128)(2,1)S(1)}, u32[]{:S(2)}, u32[]{:S(2)}) %collective-permute-start.2) | collective-permute-done | bytes 262176 | tf_op jit(solution)/shard_map/ppermute | solution.py:14
  101.6 1.5 pad_maximum_fusion.1
  103.1 3.8 pad_maximum_fusion
  106.9 1.3 broadcast.76.clone
  108.9 1.3 fusion.48
  110.2 6.4 %collective-permute-start.4 = (f32[2,1024,64]{1,2,0:T(8,128)S(1)}, f32[2,1024,64]{1,2,0:T(8,128)S(1)}, u32[]{:S(2)}, u32[]{:S(2)}) collective-permute-start(f32[2,1024,64]{1,2,0:T(8,128)S(1)} %get-tuple-element.272), channel_id=1, source_target_pairs={{0,2},{2,4},{4,6},{6,8},{8,10},{10,12},{12,14},{14,16},{16,18},{18... | collective-permute-start | bytes 1572872 | tf_op jit(solution)/shard_map/ppermute | solution.py:14
  116.6 72.9 %collective-permute-start.5 = (f32[2,1024,64]{1,2,0:T(8,128)S(1)}, f32[2,1024,64]{1,2,0:T(8,128)S(1)}, u32[]{:S(2)}, u32[]{:S(2)}) collective-permute-start(f32[2,1024,64]{1,2,0:T(8,128)S(1)} %get-tuple-element.273), channel_id=1, source_target_pairs={{0,4},{2,6},{4,8},{6,10},{8,12},{10,14},{12,16},{14,18},{16,20},{1... | collective-permute-start | bytes 1572872 | tf_op jit(solution)/shard_map/ppermute | solution.py:14
  189.5 6.1 %collective-permute-done.5 = f32[2,1024,64]{1,2,0:T(8,128)S(1)} collective-permute-done((f32[2,1024,64]{1,2,0:T(8,128)S(1)}, f32[2,1024,64]{1,2,0:T(8,128)S(1)}, u32[]{:S(2)}, u32[]{:S(2)}) %collective-permute-start.5) | collective-permute-done | bytes 524320 | tf_op jit(solution)/shard_map/ppermute | solution.py:14
  197.7 36.3 %reduce-scatter.3.cloned.1.call-done = f32[1024,64]{0,1:T(8,128)} async-done(((f32[2048,64]{0,1:T(8,128)}), f32[1024,64]{0,1:T(8,128)}) %reduce-scatter.3.cloned.1.call-update) | async-done | bytes 262160 | tf_op jit(solution)/shard_map/reduce_scatter | solution.py:101
  234.0 1.4 fusion.49
  235.5 77.5 %psum.14 = f32[64,64]{0,1:T(8,128)S(1)} all-reduce(f32[64,64]{0,1:T(8,128)S(1)} %fusion.49), channel_id=1, replica_groups=mesh['rows'=128,'cols'=2] {'rows','cols'}, use_global_device_ids=true, to_apply=%region_7.8 | all-reduce | flops 4096 | bytes 32768 | tf_op jit(solution)/shard_map/psum | solution.py:56
  313.1 5.8 %cholesky.44 = f32[64,64]{1,0:T(8,128)S(1)} custom-call(f32[64,64]{1,0:T(8,128)S(1)} %fusion.39), custom_call_target="Cholesky" | custom-call | tf_op jit(solution)/shard_map/jit(cholesky)/cholesky | solution.py:57
  320.3 4.9 custom-call.6
  325.2 1.4 fusion.34
  326.6 2.5 all_gather.3
  329.4 1.3 collective-permute-start.6
  330.7 1.3 collective-permute-start.7
  332.0 22.3 %collective-permute-done.6 = bf16[2,1024,64]{2,1,0:T(8,128)(2,1)S(1)} collective-permute-done((bf16[2,1024,64]{2,1,0:T(8,128)(2,1)S(1)}, bf16[2,1024,64]{2,1,0:T(8,128)(2,1)S(1)}, u32[]{:S(2)}, u32[]{:S(2)}) %collective-permute-start.6) | collective-permute-done | bytes 262176 | tf_op jit(solution)/shard_map/ppermute | solution.py:14
  354.2 1.5 pad_maximum_fusion.2
  355.8 1.3 broadcast.76
  357.7 1.3 fusion.47
  359.1 3.7 collective-permute-start.8
  362.7 45.1 %collective-permute-start.9 = (f32[2,1024,64]{1,2,0:T(8,128)S(1)}, f32[2,1024,64]{1,2,0:T(8,128)S(1)}, u32[]{:S(2)}, u32[]{:S(2)}) collective-permute-start(f32[2,1024,64]{1,2,0:T(8,128)S(1)} %get-tuple-element.271), channel_id=1, source_target_pairs={{0,4},{2,6},{4,8},{6,10},{8,12},{10,14},{12,16},{14,18},{16,20},{1... | collective-permute-start | bytes 1572872 | tf_op jit(solution)/shard_map/ppermute | solution.py:14
  407.8 11.5 %collective-permute-done.9 = f32[2,1024,64]{1,2,0:T(8,128)S(1)} collective-permute-done((f32[2,1024,64]{1,2,0:T(8,128)S(1)}, f32[2,1024,64]{1,2,0:T(8,128)S(1)}, u32[]{:S(2)}, u32[]{:S(2)}) %collective-permute-start.9) | collective-permute-done | bytes 524320 | tf_op jit(solution)/shard_map/ppermute | solution.py:14
  421.3 25.8 %reduce-scatter.5.cloned.1.call-done = f32[1024,64]{0,1:T(8,128)} async-done(((f32[2048,64]{0,1:T(8,128)}), f32[1024,64]{0,1:T(8,128)}) %reduce-scatter.5.cloned.1.call-update) | async-done | bytes 262160 | tf_op jit(solution)/shard_map/reduce_scatter | solution.py:101
  447.1 1.4 fusion.50
  448.4 77.5 %psum.15 = f32[64,64]{0,1:T(8,128)S(1)} all-reduce(f32[64,64]{0,1:T(8,128)S(1)} %fusion.50), channel_id=1, replica_groups=mesh['rows'=128,'cols'=2] {'rows','cols'}, use_global_device_ids=true, to_apply=%region_15.18 | all-reduce | flops 4096 | bytes 32768 | tf_op jit(solution)/shard_map/psum | solution.py:56
  526.1 5.8 %cholesky.55 = f32[64,64]{1,0:T(8,128)S(1)} custom-call(f32[64,64]{1,0:T(8,128)S(1)} %fusion.37), custom_call_target="Cholesky" | custom-call | tf_op jit(solution)/shard_map/jit(cholesky)/cholesky | solution.py:57
  533.3 4.9 custom-call.7
  538.9 2.1 convolution_bitcast_fusion.2
  (43 shorter events, 14.4 us)
Async XLA Ops:
  7.2 2.0 copy-start
  7.2 226.9 %reduce-scatter.3.cloned.1.call-start = ((), (), s32[]{:S(2)}) async-start(), calls=%async_computation.2 | async-start | bytes 786432 | tf_op jit(solution)/shard_map/reduce_scatter | solution.py:101
  9.1 3.0 copy-start.1
  9.2 5.9 %copy-start.2 = (s32[4,2]{0,1:T(2,128)S(1)}, s32[4,2]{0,1:T(2,128)}, u32[]{:S(2)}) copy-start(s32[4,2]{0,1:T(2,128)} %param.16) | copy-start | bytes 100
  9.5 93.6 %collective-permute-start = (bf16[2,1024,384]{2,1,0:T(8,128)(2,1)S(1)}, bf16[2,1024,384]{2,1,0:T(8,128)(2,1)}, u32[]{:S(2)}, u32[]{:S(2)}) collective-permute-start(bf16[2,1024,384]{2,1,0:T(8,128)(2,1)S(1)} %bitcast.145), channel_id=1, source_target_pairs={{2,0},{4,2},{6,4},{8,6},{10,8},{12,10},{14,12},{16,14},{18,16},{20... | collective-permute-start | bytes 4718600 | tf_op jit(solution)/shard_map/ppermute | solution.py:14
  10.8 92.3 %collective-permute-start.1 = (bf16[2,1024,384]{2,1,0:T(8,128)(2,1)S(1)}, bf16[2,1024,384]{2,1,0:T(8,128)(2,1)}, u32[]{:S(2)}, u32[]{:S(2)}) collective-permute-start(bf16[2,1024,384]{2,1,0:T(8,128)(2,1)S(1)} %bitcast.146), channel_id=1, source_target_pairs={{4,0},{6,2},{8,4},{10,6},{12,8},{14,10},{16,12},{18,14},{20,16},{2... | collective-permute-start | bytes 4718600 | tf_op jit(solution)/shard_map/ppermute | solution.py:14
  12.4 89.2 %collective-permute-start.2 = (bf16[2,1024,64]{2,1,0:T(8,128)(2,1)S(1)}, bf16[2,1024,64]{2,1,0:T(8,128)(2,1)S(1)}, u32[]{:S(2)}, u32[]{:S(2)}) collective-permute-start(bf16[2,1024,64]{2,1,0:T(8,128)(2,1)S(1)} %bitcast.150), channel_id=1, source_target_pairs={{2,0},{4,2},{6,4},{8,6},{10,8},{12,10},{14,12},{16,14},{18,16},{20... | collective-permute-start | bytes 786440 | tf_op jit(solution)/shard_map/ppermute | solution.py:14
  13.7 87.9 %collective-permute-start.3 = (bf16[2,1024,64]{2,1,0:T(8,128)(2,1)S(1)}, bf16[2,1024,64]{2,1,0:T(8,128)(2,1)S(1)}, u32[]{:S(2)}, u32[]{:S(2)}) collective-permute-start(bf16[2,1024,64]{2,1,0:T(8,128)(2,1)S(1)} %bitcast.151), channel_id=1, source_target_pairs={{4,0},{6,2},{8,4},{10,6},{12,8},{14,10},{16,12},{18,14},{20,16},{2... | collective-permute-start | bytes 786440 | tf_op jit(solution)/shard_map/ppermute | solution.py:14
  110.2 79.3 %collective-permute-start.4 = (f32[2,1024,64]{1,2,0:T(8,128)S(1)}, f32[2,1024,64]{1,2,0:T(8,128)S(1)}, u32[]{:S(2)}, u32[]{:S(2)}) collective-permute-start(f32[2,1024,64]{1,2,0:T(8,128)S(1)} %get-tuple-element.272), channel_id=1, source_target_pairs={{0,2},{2,4},{4,6},{6,8},{8,10},{10,12},{12,14},{14,16},{16,18},{18... | collective-permute-start | bytes 1572872 | tf_op jit(solution)/shard_map/ppermute | solution.py:14
  116.6 79.0 %collective-permute-start.5 = (f32[2,1024,64]{1,2,0:T(8,128)S(1)}, f32[2,1024,64]{1,2,0:T(8,128)S(1)}, u32[]{:S(2)}, u32[]{:S(2)}) collective-permute-start(f32[2,1024,64]{1,2,0:T(8,128)S(1)} %get-tuple-element.273), channel_id=1, source_target_pairs={{0,4},{2,6},{4,8},{6,10},{8,12},{10,14},{12,16},{14,18},{16,20},{1... | collective-permute-start | bytes 1572872 | tf_op jit(solution)/shard_map/ppermute | solution.py:14
  197.7 249.4 %reduce-scatter.5.cloned.1.call-start = ((), (), s32[]{:S(2)}) async-start(), calls=%async_computation.3 | async-start | bytes 786432 | tf_op jit(solution)/shard_map/reduce_scatter | solution.py:101
  329.4 24.9 %collective-permute-start.6 = (bf16[2,1024,64]{2,1,0:T(8,128)(2,1)S(1)}, bf16[2,1024,64]{2,1,0:T(8,128)(2,1)S(1)}, u32[]{:S(2)}, u32[]{:S(2)}) collective-permute-start(bf16[2,1024,64]{2,1,0:T(8,128)(2,1)S(1)} %bitcast.153), channel_id=1, source_target_pairs={{2,0},{4,2},{6,4},{8,6},{10,8},{12,10},{14,12},{16,14},{18,16},{20... | collective-permute-start | bytes 786440 | tf_op jit(solution)/shard_map/ppermute | solution.py:14
  330.7 23.6 %collective-permute-start.7 = (bf16[2,1024,64]{2,1,0:T(8,128)(2,1)S(1)}, bf16[2,1024,64]{2,1,0:T(8,128)(2,1)S(1)}, u32[]{:S(2)}, u32[]{:S(2)}) collective-permute-start(bf16[2,1024,64]{2,1,0:T(8,128)(2,1)S(1)} %bitcast.154), channel_id=1, source_target_pairs={{4,0},{6,2},{8,4},{10,6},{12,8},{14,10},{16,12},{18,14},{20,16},{2... | collective-permute-start | bytes 786440 | tf_op jit(solution)/shard_map/ppermute | solution.py:14
  359.1 48.8 %collective-permute-start.8 = (f32[2,1024,64]{1,2,0:T(8,128)S(1)}, f32[2,1024,64]{1,2,0:T(8,128)S(1)}, u32[]{:S(2)}, u32[]{:S(2)}) collective-permute-start(f32[2,1024,64]{1,2,0:T(8,128)S(1)} %get-tuple-element.270), channel_id=1, source_target_pairs={{0,2},{2,4},{4,6},{6,8},{8,10},{10,12},{12,14},{14,16},{16,18},{18... | collective-permute-start | bytes 1572872 | tf_op jit(solution)/shard_map/ppermute | solution.py:14
  362.7 56.6 %collective-permute-start.9 = (f32[2,1024,64]{1,2,0:T(8,128)S(1)}, f32[2,1024,64]{1,2,0:T(8,128)S(1)}, u32[]{:S(2)}, u32[]{:S(2)}) collective-permute-start(f32[2,1024,64]{1,2,0:T(8,128)S(1)} %get-tuple-element.271), channel_id=1, source_target_pairs={{0,4},{2,6},{4,8},{6,10},{8,12},{10,14},{12,16},{14,18},{16,20},{1... | collective-permute-start | bytes 1572872 | tf_op jit(solution)/shard_map/ppermute | solution.py:14
Sparse Core Ops, SparseCore 0:
  197.8 36.2 reduce-scatter.2
  421.4 25.5 reduce-scatter.4
where the time goes:
time: 550 us; the launch traced here: 548 us
  waiting for transfers between devices  188 us (34%)
  blocking collectives  158 us (29%)
  starting transfers between devices  136 us (25%)
  other arithmetic  36.2 us (7%)
  between operations  14.3 us (3%)
  local copies, waits for them, and re-layouts  8.38 us (2%)
  matrix products  6.27 us (1%)
    psum x2, blocking collectives, orthonormal(): gram_matrix = lax.psum(gram_matrix, ('rows', 'cols')) / rows_total  155 us
    ppermute x10, starting transfers between devices, shifted(): lax.ppermute(value, axis, [(source, source + steps) for source in range(i...  136 us
    ppermute x10, waiting for transfers between devices, shifted(): lax.ppermute(value, axis, [(source, source + steps) for source in range(i...  126 us
    reduce_scatter x2, waiting for transfers between devices, affinity_pass(): return lax.psum_scatter(flattened, 'cols', scatter_dimension=0, tiled=True)  62.1 us
    another operation x6, other arithmetic, orthonormal(): lower_factor = jnp.linalg.cholesky(gram_matrix)  13 us
  transfers between devices with their start and end apart: 12, of which 6 were waited for; matrix products, arithmetic and copies ran while one was open for 0% of the time, Pallas kernels for 0%

commit v1 on v0

--- a/solution.py
+++ b/solution.py
@@ -2,6 +2,7 @@
 import jax.numpy as jnp
 from jax import lax
 from jax.sharding import PartitionSpec as P
+from jax.lax import all_gather
 
 BLK = 1024
 SHARPNESS = 6.0
@@ -53,7 +54,7 @@
         precision=lax.Precision.HIGHEST,
         preferred_element_type=jnp.float32,
     )
-    gram_matrix = lax.psum(gram_matrix, ("rows", "cols")) / rows_total
+    gram_matrix = jnp.sum(all_gather(gram_matrix, ("rows", "cols")), axis=0) / rows_total
     lower_factor = jnp.linalg.cholesky(gram_matrix)
     solved = lax.linalg.triangular_solve(
         lower_factor, sketch_rows, left_side=False, lower=True, transpose_a=True

time: 550 us -> 647 us (1.18)
  waiting for transfers between devices: 188 us -> 429 us
  blocking collectives: 158 us -> 1.99 us
  other arithmetic: 36.2 us -> 44.2 us
    all_gather x0 -> x2, waiting for transfers between devices: none -> 243 us  [orthonormal(): all_gather(gram_matrix, ('rows', 'cols'))]
    psum x2 -> x0, blocking collectives: 155 us -> none  [orthonormal(): gram_matrix = lax.psum(gram_matrix, ('rows', 'cols')) / rows_total]
    reduce_sum x0 -> x2, other arithmetic: none -> 8.11 us  [orthonormal(): jnp.sum(all_gather(gram_matrix, ('rows', 'cols')), axis=0) / rows_total]
  transfers between devices with their start and end apart: 12 -> 14, of which waited for: 6 -> 8; matrix products, arithmetic and copies ran while one was open for 0% -> 0% of each run, Pallas kernels for 0% -> 0%
where the time goes in v1:
time: 647 us; the launch traced here: 645 us
  waiting for transfers between devices  429 us (66%)
  starting transfers between devices  140 us (22%)
  other arithmetic  44.2 us (7%)
  between operations  14.1 us (2%)
  local copies, waits for them, and re-layouts  8.58 us (1%)
    all_gather x2, waiting for transfers between devices, orthonormal(): all_gather(gram_matrix, ('rows', 'cols'))  243 us
    ppermute x10, starting transfers between devices, shifted(): lax.ppermute(value, axis, [(source, source + steps) for source in range(i...  140 us
    ppermute x10, waiting for transfers between devices, shifted(): lax.ppermute(value, axis, [(source, source + steps) for source in range(i...  124 us
    reduce_scatter x2, waiting for transfers between devices, affinity_pass(): return lax.psum_scatter(flattened, 'cols', scatter_dimension=0, tiled=True)  61.4 us
    another operation x6, other arithmetic, orthonormal(): lower_factor = jnp.linalg.cholesky(gram_matrix)  13 us
  transfers between devices with their start and end apart: 14, of which 8 were waited for; matrix products, arithmetic and copies ran while one was open for 0% of the time, Pallas kernels for 0%

profile of v1, /device:TPU:1, one launch (start us, length us, event | category | flops | bytes accessed | tf_op | source)
XLA Modules:
  0.0 644.7 jit_solution(16288063069667614076)
XLA Ops:
  7.2 1.9 fusion.32
  9.5 1.3 collective-permute-start
  10.8 1.3 collective-permute-start.1
  12.4 1.3 collective-permute-start.2
  15.7 85.9 %collective-permute-done.2 = bf16[2,1024,64]{2,1,0:T(8,128)(2,1)S(1)} collective-permute-done((bf16[2,1024,64]{2,1,0:T(8,128)(2,1)S(1)}, bf16[2,1024,64]{2,1,0:T(8,128)(2,1)S(1)}, u32[]{:S(2)}, u32[]{:S(2)}) %collective-permute-start.2) | collective-permute-done | bytes 262176 | tf_op jit(solution)/shard_map/ppermute | solution.py:15
  101.6 1.5 pad_maximum_fusion.1
  103.1 3.8 pad_maximum_fusion
  106.9 1.3 broadcast.76.clone
  108.9 1.3 fusion.48
  110.2 6.4 collective-permute-start.4
  116.6 72.7 %collective-permute-start.5 = (f32[2,1024,64]{1,2,0:T(8,128)S(1)}, f32[2,1024,64]{1,2,0:T(8,128)S(1)}, u32[]{:S(2)}, u32[]{:S(2)}) collective-permute-start(f32[2,1024,64]{1,2,0:T(8,128)S(1)} %get-tuple-element.275), channel_id=1, source_target_pairs={{0,4},{2,6},{4,8},{6,10},{8,12},{10,14},{12,16},{14,18},{16,20},{1... | collective-permute-start | bytes 1572872 | tf_op jit(solution)/shard_map/ppermute | solution.py:15
  189.3 6.1 collective-permute-done.5
  197.4 36.4 %reduce-scatter.3.cloned.1.call-done = f32[1024,64]{0,1:T(8,128)} async-done(((f32[2048,64]{0,1:T(8,128)}), f32[1024,64]{0,1:T(8,128)}) %reduce-scatter.3.cloned.1.call-update) | async-done | bytes 262160 | tf_op jit(solution)/shard_map/reduce_scatter | solution.py:102
  233.8 2.0 fusion.49
  235.9 122.1 %all-gather.5.cloned.1.call-done = f32[16384,64]{1,0:T(8,128)} async-done(((f32[64,64]{1,0:T(8,128)}), f32[16384,64]{1,0:T(8,128)}) %all-gather.5.cloned.1.call-update) | async-done | bytes 4194320 | tf_op jit(solution)/shard_map/all_gather | solution.py:57
  358.0 4.1 reduce_sum.42
  362.2 5.8 cholesky.44
  369.4 4.9 custom-call.6
  374.7 2.0 all_gather.17
  379.6 20.4 %collective-permute-done.6 = bf16[2,1024,64]{2,1,0:T(8,128)(2,1)S(1)} collective-permute-done((bf16[2,1024,64]{2,1,0:T(8,128)(2,1)S(1)}, bf16[2,1024,64]{2,1,0:T(8,128)(2,1)S(1)}, u32[]{:S(2)}, u32[]{:S(2)}) %collective-permute-start.6) | collective-permute-done | bytes 262176 | tf_op jit(solution)/shard_map/ppermute | solution.py:15
  400.0 1.5 pad_maximum_fusion.2
  401.5 1.3 broadcast.76
  403.5 1.3 fusion.47
  404.8 7.5 %collective-permute-start.8 = (f32[2,1024,64]{1,2,0:T(8,128)S(1)}, f32[2,1024,64]{1,2,0:T(8,128)S(1)}, u32[]{:S(2)}, u32[]{:S(2)}) collective-permute-start(f32[2,1024,64]{1,2,0:T(8,128)S(1)} %get-tuple-element.272), channel_id=1, source_target_pairs={{0,2},{2,4},{4,6},{6,8},{8,10},{10,12},{12,14},{14,16},{16,18},{18... | collective-permute-start | bytes 1572872 | tf_op jit(solution)/shard_map/ppermute | solution.py:15
  412.3 45.2 %collective-permute-start.9 = (f32[2,1024,64]{1,2,0:T(8,128)S(1)}, f32[2,1024,64]{1,2,0:T(8,128)S(1)}, u32[]{:S(2)}, u32[]{:S(2)}) collective-permute-start(f32[2,1024,64]{1,2,0:T(8,128)S(1)} %get-tuple-element.273), channel_id=1, source_target_pairs={{0,4},{2,6},{4,8},{6,10},{8,12},{10,14},{12,16},{14,18},{16,20},{1... | collective-permute-start | bytes 1572872 | tf_op jit(solution)/shard_map/ppermute | solution.py:15
  457.5 11.8 %collective-permute-done.9 = f32[2,1024,64]{1,2,0:T(8,128)S(1)} collective-permute-done((f32[2,1024,64]{1,2,0:T(8,128)S(1)}, f32[2,1024,64]{1,2,0:T(8,128)S(1)}, u32[]{:S(2)}, u32[]{:S(2)}) %collective-permute-start.9) | collective-permute-done | bytes 524320 | tf_op jit(solution)/shard_map/ppermute | solution.py:15
  471.6 25.0 %reduce-scatter.5.cloned.1.call-done = f32[1024,64]{0,1:T(8,128)} async-done(((f32[2048,64]{0,1:T(8,128)}), f32[1024,64]{0,1:T(8,128)}) %reduce-scatter.5.cloned.1.call-update) | async-done | bytes 262160 | tf_op jit(solution)/shard_map/reduce_scatter | solution.py:102
  496.6 2.0 fusion.50
  498.6 121.4 %all-gather.7.cloned.1.call-done = f32[16384,64]{1,0:T(8,128)} async-done(((f32[64,64]{1,0:T(8,128)}), f32[16384,64]{1,0:T(8,128)}) %all-gather.7.cloned.1.call-update) | async-done | bytes 4194320 | tf_op jit(solution)/shard_map/all_gather | solution.py:57
  620.0 4.1 reduce_sum.43
  624.3 5.8 cholesky.55
  631.4 4.9 custom-call.7
  (55 shorter events, 16.4 us)
Async XLA Ops:
  7.2 2.0 copy-start
  7.2 226.6 %reduce-scatter.3.cloned.1.call-start = ((), (), s32[]{:S(2)}) async-start(), calls=%async_computation.2 | async-start | bytes 786432 | tf_op jit(solution)/shard_map/reduce_scatter | solution.py:102
  9.1 3.0 copy-start.3
  9.2 5.9 copy-start.4
  9.5 93.6 %collective-permute-start = (bf16[2,1024,384]{2,1,0:T(8,128)(2,1)S(1)}, bf16[2,1024,384]{2,1,0:T(8,128)(2,1)}, u32[]{:S(2)}, u32[]{:S(2)}) collective-permute-start(bf16[2,1024,384]{2,1,0:T(8,128)(2,1)S(1)} %bitcast.149), channel_id=1, source_target_pairs={{2,0},{4,2},{6,4},{8,6},{10,8},{12,10},{14,12},{16,14},{18,16},{20... | collective-permute-start | bytes 4718600 | tf_op jit(solution)/shard_map/ppermute | solution.py:15
  10.8 92.3 %collective-permute-start.1 = (bf16[2,1024,384]{2,1,0:T(8,128)(2,1)S(1)}, bf16[2,1024,384]{2,1,0:T(8,128)(2,1)}, u32[]{:S(2)}, u32[]{:S(2)}) collective-permute-start(bf16[2,1024,384]{2,1,0:T(8,128)(2,1)S(1)} %bitcast.150), channel_id=1, source_target_pairs={{4,0},{6,2},{8,4},{10,6},{12,8},{14,10},{16,12},{18,14},{20,16},{2... | collective-permute-start | bytes 4718600 | tf_op jit(solution)/shard_map/ppermute | solution.py:15
  12.4 89.2 %collective-permute-start.2 = (bf16[2,1024,64]{2,1,0:T(8,128)(2,1)S(1)}, bf16[2,1024,64]{2,1,0:T(8,128)(2,1)S(1)}, u32[]{:S(2)}, u32[]{:S(2)}) collective-permute-start(bf16[2,1024,64]{2,1,0:T(8,128)(2,1)S(1)} %bitcast.154), channel_id=1, source_target_pairs={{2,0},{4,2},{6,4},{8,6},{10,8},{12,10},{14,12},{16,14},{18,16},{20... | collective-permute-start | bytes 786440 | tf_op jit(solution)/shard_map/ppermute | solution.py:15
  13.7 87.9 %collective-permute-start.3 = (bf16[2,1024,64]{2,1,0:T(8,128)(2,1)S(1)}, bf16[2,1024,64]{2,1,0:T(8,128)(2,1)S(1)}, u32[]{:S(2)}, u32[]{:S(2)}) collective-permute-start(bf16[2,1024,64]{2,1,0:T(8,128)(2,1)S(1)} %bitcast.155), channel_id=1, source_target_pairs={{4,0},{6,2},{8,4},{10,6},{12,8},{14,10},{16,12},{18,14},{20,16},{2... | collective-permute-start | bytes 786440 | tf_op jit(solution)/shard_map/ppermute | solution.py:15
  110.2 79.1 %collective-permute-start.4 = (f32[2,1024,64]{1,2,0:T(8,128)S(1)}, f32[2,1024,64]{1,2,0:T(8,128)S(1)}, u32[]{:S(2)}, u32[]{:S(2)}) collective-permute-start(f32[2,1024,64]{1,2,0:T(8,128)S(1)} %get-tuple-element.274), channel_id=1, source_target_pairs={{0,2},{2,4},{4,6},{6,8},{8,10},{10,12},{12,14},{14,16},{16,18},{18... | collective-permute-start | bytes 1572872 | tf_op jit(solution)/shard_map/ppermute | solution.py:15
  116.6 78.8 %collective-permute-start.5 = (f32[2,1024,64]{1,2,0:T(8,128)S(1)}, f32[2,1024,64]{1,2,0:T(8,128)S(1)}, u32[]{:S(2)}, u32[]{:S(2)}) collective-permute-start(f32[2,1024,64]{1,2,0:T(8,128)S(1)} %get-tuple-element.275), channel_id=1, source_target_pairs={{0,4},{2,6},{4,8},{6,10},{8,12},{10,14},{12,16},{14,18},{16,20},{1... | collective-permute-start | bytes 1572872 | tf_op jit(solution)/shard_map/ppermute | solution.py:15
  197.4 160.6 %all-gather.5.cloned.1.call-start = ((), (), s32[]{:S(2)}) async-start(), calls=%async_computation.4 | async-start | bytes 8421376 | tf_op jit(solution)/shard_map/all_gather | solution.py:57
  235.8 260.8 %reduce-scatter.5.cloned.1.call-start = ((), (), s32[]{:S(2)}) async-start(), calls=%async_computation.3 | async-start | bytes 786432 | tf_op jit(solution)/shard_map/reduce_scatter | solution.py:102
  358.0 16.3 %copy-start.2 = (f32[1024,64]{0,1:T(8,128)S(1)}, f32[1024,64]{0,1:T(8,128)}, u32[]{:S(2)}) copy-start(f32[1024,64]{0,1:T(8,128)} %reduce-scatter.3.cloned.1.call-done) | copy-start | bytes 786436
  377.0 23.0 %collective-permute-start.6 = (bf16[2,1024,64]{2,1,0:T(8,128)(2,1)S(1)}, bf16[2,1024,64]{2,1,0:T(8,128)(2,1)S(1)}, u32[]{:S(2)}, u32[]{:S(2)}) collective-permute-start(bf16[2,1024,64]{2,1,0:T(8,128)(2,1)S(1)} %bitcast.157), channel_id=1, source_target_pairs={{2,0},{4,2},{6,4},{8,6},{10,8},{12,10},{14,12},{16,14},{18,16},{20... | collective-permute-start | bytes 786440 | tf_op jit(solution)/shard_map/ppermute | solution.py:15
  378.3 21.7 %collective-permute-start.7 = (bf16[2,1024,64]{2,1,0:T(8,128)(2,1)S(1)}, bf16[2,1024,64]{2,1,0:T(8,128)(2,1)S(1)}, u32[]{:S(2)}, u32[]{:S(2)}) collective-permute-start(bf16[2,1024,64]{2,1,0:T(8,128)(2,1)S(1)} %bitcast.158), channel_id=1, source_target_pairs={{4,0},{6,2},{8,4},{10,6},{12,8},{14,10},{16,12},{18,14},{20,16},{2... | collective-permute-start | bytes 786440 | tf_op jit(solution)/shard_map/ppermute | solution.py:15
  404.8 52.8 %collective-permute-start.8 = (f32[2,1024,64]{1,2,0:T(8,128)S(1)}, f32[2,1024,64]{1,2,0:T(8,128)S(1)}, u32[]{:S(2)}, u32[]{:S(2)}) collective-permute-start(f32[2,1024,64]{1,2,0:T(8,128)S(1)} %get-tuple-element.272), channel_id=1, source_target_pairs={{0,2},{2,4},{4,6},{6,8},{8,10},{10,12},{12,14},{14,16},{16,18},{18... | collective-permute-start | bytes 1572872 | tf_op jit(solution)/shard_map/ppermute | solution.py:15
  412.3 57.1 %collective-permute-start.9 = (f32[2,1024,64]{1,2,0:T(8,128)S(1)}, f32[2,1024,64]{1,2,0:T(8,128)S(1)}, u32[]{:S(2)}, u32[]{:S(2)}) collective-permute-start(f32[2,1024,64]{1,2,0:T(8,128)S(1)} %get-tuple-element.273), channel_id=1, source_target_pairs={{0,4},{2,6},{4,8},{6,10},{8,12},{10,14},{12,16},{14,18},{16,20},{1... | collective-permute-start | bytes 1572872 | tf_op jit(solution)/shard_map/ppermute | solution.py:15
  471.3 148.7 %all-gather.7.cloned.1.call-start = ((), (), s32[]{:S(2)}) async-start(), calls=%async_computation.5 | async-start | bytes 8421376 | tf_op jit(solution)/shard_map/all_gather | solution.py:57
  620.0 17.0 %copy-start.1 = (f32[1024,64]{0,1:T(8,128)S(1)}, f32[1024,64]{0,1:T(8,128)}, u32[]{:S(2)}) copy-start(f32[1024,64]{0,1:T(8,128)} %reduce-scatter.5.cloned.1.call-done) | copy-start | bytes 786436
Sparse Core Ops, SparseCore 0:
  197.5 36.2 reduce-scatter.2
  238.7 119.2 all-gather.4
  471.5 25.0 reduce-scatter.4
  500.7 119.2 all-gather.6
